TPU v7x, 32 devices: a whole 2x2x4 slice. The times are simulated.
32 devices in a mesh: groups: 2 (over x), items: 16 (over z, y, core).
Axes of the slice: x: 2, y: 2, z: 4, core: 2. Of those that a mesh axis runs over, the one named last changes fastest.
Arguments:
- candidate_traits: bfloat16 [16384, 2048], P(('groups', 'items')), parts along dimension 0, may hold values from -6 to 6
- candidate_tower_matrix: bfloat16 [2048, 512], replicated, may hold values from -0.125 to 0.125
- query_vectors: bfloat16 [128, 512], P(('groups', 'items')), parts along dimension 0, may hold values from -6 to 6
- kept_positions: int32 [128, 128], P('groups', 'items'), parts along dimension 0, may hold values from 0 to 511
- ranker_first_matrix: bfloat16 [1024, 1024], replicated, may hold values from -0.1875 to 0.1875
- ranker_second_matrix: bfloat16 [1024, 1024], replicated, may hold values from -0.1875 to 0.1875
- ranker_final_vector: bfloat16 [1024], replicated, may hold values from -0.1875 to 0.1875
Outputs:
- prescore: float32 [16384, 64], P(('groups', 'items')), parts along dimension 0
- ranking: float32 [128, 128], P(('groups', 'items')), parts along dimension 0
There are 2 independent parts, one for each index of `groups`. A program takes and returns all parts, laid end to end along the dimension named above; an argument that names none is the same for every part. Nothing has to cross between parts.
Inputs may be any that keep to these rules, and one draw needn't show every extreme that they name: `kept_positions`: entry j of a request is a position within item shard j // 8, which holds items j // 8 * 512 onward.
All inputs are finite; a program needn't handle non-finite values.
Results may differ from a plain program's by a relative error of at most 0.013.
Values may be sent and summed in bfloat16 or wider, within the bound.
A program may use at most 64 MiB of HBM per device.

v0:
```python
import jax
import jax.numpy as jnp
from jax import lax
from jax.sharding import PartitionSpec as P


def item_tower(candidate_traits, candidate_tower_matrix):
    raw = jnp.dot(candidate_traits, candidate_tower_matrix, preferred_element_type=jnp.float32)
    factor = lax.rsqrt(jnp.mean(raw * raw, axis=-1, keepdims=True) + 1e-06)
    return (raw * factor).astype(jnp.bfloat16)


def cross_tower(
    item_rows, user_rows, ranker_first_matrix, ranker_second_matrix, ranker_final_vector
):
    owned, count, width = item_rows.shape
    product = (item_rows.astype(jnp.float32) * user_rows.astype(jnp.float32)[:, None, :]).astype(
        jnp.bfloat16
    )
    cross_in = jnp.concatenate([product, item_rows], axis=-1).reshape(owned * count, 2 * width)
    hidden_one = jax.nn.silu(
        jnp.dot(cross_in, ranker_first_matrix, preferred_element_type=jnp.float32)
    ).astype(jnp.bfloat16)
    hidden_two = jax.nn.silu(
        jnp.dot(hidden_one, ranker_second_matrix, preferred_element_type=jnp.float32)
    ).astype(jnp.bfloat16)
    return jnp.dot(hidden_two, ranker_final_vector, preferred_element_type=jnp.float32).reshape(
        owned, count
    )


def per_device(
    candidate_traits,
    candidate_tower_matrix,
    query_vectors,
    kept_positions,
    ranker_first_matrix,
    ranker_second_matrix,
    ranker_final_vector,
):
    candidate_vectors = item_tower(candidate_traits, candidate_tower_matrix)
    width = candidate_vectors.shape[1]
    all_users = lax.all_gather(query_vectors, "items", axis=0, tiled=True)
    prescore = lax.dot_general(
        candidate_vectors, all_users, (((1,), (1,)), ((), ())), preferred_element_type=jnp.float32
    ) * width ** (-0.5)
    selected_candidates = jnp.take(candidate_vectors, kept_positions, axis=0)
    item_rows = lax.all_to_all(
        selected_candidates, "items", split_axis=0, concat_axis=1, tiled=True
    )
    ranking = cross_tower(
        item_rows, query_vectors, ranker_first_matrix, ranker_second_matrix, ranker_final_vector
    )
    return (prescore, ranking)


def solution(mesh):
    placed = (
        P(("groups", "items"), None),
        P(),
        P(("groups", "items"), None),
        P("groups", "items"),
        P(),
        P(),
        P(),
    )
    return jax.shard_map(
        per_device,
        mesh=mesh,
        in_specs=placed,
        out_specs=(P(("groups", "items"), None), P(("groups", "items"), None)),
        check_vma=False,
    )
```

profile of v0, /device:TPU:0, one launch (start us, length us, event | category | flops | bytes accessed | tf_op | source)
XLA Modules:
  0.0 51.8 jit_solution(16912730754630676367)
XLA Ops:
  0.6 0.0 copy-start
  0.6 0.8 %compare_and_fusion = pred[64,8]{0,1:T(8,128)(4,1)S(1)} fusion(s32[64,8]{0,1:T(8,128)} %param.10), kind=kLoop, calls=%fused_computation.18 | loop fusion | flops 3072 | bytes 2560 | tf_op jit(solution)/shard_map/jit(_take)/and | solution.py:47
  1.5 0.7 %compare_select_fusion = s32[64,8]{0,1:T(8,128)S(1)} fusion(s32[64,8]{0,1:T(8,128)} %param.10), kind=kLoop, calls=%fused_computation.16 | loop fusion | flops 1536 | bytes 4096 | tf_op jit(solution)/shard_map/jit(_take)/jit(_where)/select_n | solution.py:47
  2.2 0.1 copy.18
  2.3 0.1 copy.19
  2.4 0.1 reshape.30
  2.5 3.5 %multiply_reduce_fusion = (f32[512]{0:T(512)S(1)}, f32[512,512]{0,1:T(8,128)S(1)}) fusion(bf16[512,2048]{1,0:T(8,128)(2,1)} %param.7, bf16[2048,512]{1,0:T(8,128)(2,1)} %param.8), kind=kOutput, calls=%fused_computation.14 | convolution fusion | flops 1074265600 | bytes 5244928 | tf_op jit(solution)/shard_map/dot_general | solution.py:8
  6.0 0.1 multiply_convert_fusion.7
  6.1 0.2 copy.20
  6.4 2.6 %gather_fusion = bf16[512,512]{1,0:T(8,128)(2,1)} fusion(bf16[512,512]{1,0:T(8,128)(2,1)S(1)} %copy.20, s32[1024]{0:T(1024)S(1)} %pad_clamp_fusion), kind=kCustom, calls=%fused_computation | custom fusion | bytes 1050624 | tf_op jit(solution)/shard_map/jit(_take)/gather | solution.py:47
  9.0 0.0 copy-start.2
  9.0 0.0 copy-start.1
  9.0 2.0 %bitcast_select_fusion = bf16[64,8,512]{2,1,0:T(8,128)(2,1)} fusion(bf16[512,512]{1,0:T(8,128)(2,1)} %gather_fusion, pred[64,8]{1,0:T(8,128)(4,1)S(1)} %copy.18), kind=kLoop, calls=%fused_computation.15 | loop fusion | flops 262144 | bytes 1049088 | tf_op jit(solution)/shard_map/jit(_take)/select_n | solution.py:47
  11.0 7.4 %all-to-all-start = ((bf16[64,8,512]{2,1,0:T(8,128)(2,1)}), bf16[64,8,512]{2,1,0:T(8,128)(2,1)S(1)}, u32[]{:S(2)}, u32[]{:S(2)}) async-start(bf16[64,8,512]{2,1,0:T(8,128)(2,1)} %bitcast_select_fusion), calls=%async_computation | async-start | bytes 1048576 | tf_op jit(solution)/shard_map/all_to_all | solution.py:48
  18.4 0.0 copy-done.2
  18.4 0.0 copy-done.1
  18.4 25.1 %all-gather = bf16[16,4,512]{2,1,0:T(4,128)(2,1)S(1)} all-gather(bf16[1,4,512]{2,1,0:T(4,128)(2,1)S(1)} %bitcast.24), channel_id=1, replica_groups=mesh['groups'=2,'items'=16] {'items'}, dimensions={0}, use_global_device_ids=true | all-gather | bytes 69632 | tf_op jit(solution)/shard_map/all_gather | solution.py:43
  43.6 0.9 %convolution_multiply_fusion = f32[512,64]{0,1:T(8,128)} fusion(bf16[64,512]{1,0:T(8,128)(2,1)S(1)} %reshape.39, bf16[512,512]{0,1:T(8,128)(2,1)S(1)} %multiply_convert_fusion.7), kind=kOutput, calls=%fused_computation.3 | convolution fusion | flops 33587200 | bytes 720896 | tf_op jit(solution)/shard_map/dot_general | solution.py:44
  44.4 0.0 all-to-all-done
  44.5 0.1 fusion.6
  44.6 0.0 copy-done
  44.6 2.6 %fusion.2 = f32[512,1024]{1,0:T(8,128)} fusion(bf16[1024,1024]{1,0:T(8,128)(2,1)S(1)} %copy-done, bf16[512,512]{1,0:T(8,128)(2,1)S(1)} %bitcast.23, bf16[512,512]{1,0:T(8,128)(2,1)S(1)} %fusion.6), kind=kOutput, calls=%fused_computation.6 | convolution fusion | flops 1075838976 | bytes 5242880 | tf_op jit(solution)/shard_map/dot_general | solution.py:22
  47.2 4.6 %fusion.1 = f32[1,512]{1,0:T(1,128)} fusion(bf16[1024,1]{0,1:T(2,128)(2,1)S(1)} %reshape.40, bf16[1024,1024]{1,0:T(8,128)(2,1)} %param.12, f32[512,1024]{1,0:T(8,128)} %fusion.2), kind=kOutput, calls=%fused_computation.5 | convolution fusion | flops 1080033280 | bytes 4198400 | tf_op jit(solution)/shard_map/dot_general | solution.py:27
  (6 shorter events, 0.1 us)
Async XLA Ops:
  0.6 44.0 %copy-start = (bf16[1024,1024]{1,0:T(8,128)(2,1)S(1)}, bf16[1024,1024]{1,0:T(8,128)(2,1)}, u32[]{:S(2)}) copy-start(bf16[1024,1024]{1,0:T(8,128)(2,1)} %param.11) | copy-start | bytes 6291460
  9.0 9.4 %copy-start.2 = (bf16[1024]{0:T(1024)(128)(2,1)S(1)}, bf16[1024]{0:T(1024)(128)(2,1)}, u32[]{:S(2)}) copy-start(bf16[1024]{0:T(1024)(128)(2,1)} %param.13) | copy-start | bytes 6148
  9.0 9.4 %copy-start.1 = (bf16[4,512]{1,0:T(4,128)(2,1)S(1)}, bf16[4,512]{1,0:T(4,128)(2,1)}, u32[]{:S(2)}) copy-start(bf16[4,512]{1,0:T(4,128)(2,1)} %param.9) | copy-start | bytes 12292
  11.0 33.5 %all-to-all-start = ((bf16[64,8,512]{2,1,0:T(8,128)(2,1)}), bf16[64,8,512]{2,1,0:T(8,128)(2,1)S(1)}, u32[]{:S(2)}, u32[]{:S(2)}) async-start(bf16[64,8,512]{2,1,0:T(8,128)(2,1)} %bitcast_select_fusion), calls=%async_computation | async-start | bytes 1048576 | tf_op jit(solution)/shard_map/all_to_all | solution.py:48
where the time goes:
time: 52.1 us; the launch traced here: 51.8 us
  blocking collectives  25.1 us (48%)
  matrix products  11.6 us (22%)
  starting transfers between devices  7.41 us (14%)
  other arithmetic  3.79 us (7%)
  local copies, waits for them, and re-layouts  3.19 us (6%)
  between operations  0.73 us (1%)
    all_gather x1, blocking collectives, per_device(): all_users = lax.all_gather(query_vectors, 'items', axis=0, tiled=True)  25.1 us
    all_to_all x1, starting transfers between devices, per_device(): lax.all_to_all(selected_candidates, 'items', split_axis=0, concat_axis=1,...  7.41 us
    dot_general x1, matrix products, cross_tower(): jnp.dot(hidden_two, ranker_final_vector, preferred_element_type=jnp.float32)  4.56 us
    dot_general x1, matrix products, item_tower(): jnp.dot(candidate_traits, candidate_tower_matrix, preferred_element_type=...  3.53 us
    select_n x2, other arithmetic, per_device(): selected_candidates = jnp.take(candidate_vectors, kept_positions, axis=0)  2.68 us
    dot_general x1, matrix products, cross_tower(): jnp.dot(cross_in, ranker_first_matrix, preferred_element_type=jnp.float32)  2.63 us
    gather x1, local copies, waits for them, and re-layouts, per_device(): selected_candidates = jnp.take(candidate_vectors, kept_positions, axis=0)  2.61 us
  transfers between devices with their start and end apart: 1, of which 0 were waited for; matrix products, arithmetic and copies ran while one was open for 2% of the time, Pallas kernels for 0%

commit v1 on v0

--- a/solution.py
+++ b/solution.py
@@ -2,6 +2,12 @@
 import jax.numpy as jnp
 from jax import lax
 from jax.sharding import PartitionSpec as P
+
+
+def swap_blocks(value, name, split, join):
+    pieces = jnp.split(value, lax.axis_size(name), axis=split)
+    got = lax.all_to_all(jnp.stack(pieces), name, 0, 0)
+    return jnp.concatenate(got, axis=join)
 
 
 def item_tower(candidate_traits, candidate_tower_matrix):
@@ -45,9 +51,7 @@
         candidate_vectors, all_users, (((1,), (1,)), ((), ())), preferred_element_type=jnp.float32
     ) * width ** (-0.5)
     selected_candidates = jnp.take(candidate_vectors, kept_positions, axis=0)
-    item_rows = lax.all_to_all(
-        selected_candidates, "items", split_axis=0, concat_axis=1, tiled=True
-    )
+    item_rows = swap_blocks(selected_candidates, "items", 0, 1)
     ranking = cross_tower(
         item_rows, query_vectors, ranker_first_matrix, ranker_second_matrix, ranker_final_vector
     )

time: 52.1 us -> 61 us (1.17)
  local copies, waits for them, and re-layouts: 3.19 us -> 12.9 us
  other arithmetic: 3.79 us -> 3.01 us
    unnamed x8 -> x23, local copies, waits for them, and re-layouts: 0.04 us -> 9.11 us
    select_n x2, other arithmetic: 2.68 us -> 1.89 us  [per_device(): selected_candidates = jnp.take(candidate_vectors, kept_positions, axis=0)]
  transfers between devices with their start and end apart: 1 -> 1, of which waited for: 0 -> 0; matrix products, arithmetic and copies ran while one was open for 2% -> 1% of each run, Pallas kernels for 0% -> 0%
where the time goes in v1:
time: 61 us; the launch traced here: 60.7 us
  blocking collectives  25.1 us (41%)
  local copies, waits for them, and re-layouts  12.9 us (21%)
  matrix products  11.5 us (19%)
  starting transfers between devices  7.41 us (12%)
  other arithmetic  3.01 us (5%)
  between operations  0.75 us (1%)
    all_gather x1, blocking collectives, per_device(): all_users = lax.all_gather(query_vectors, 'items', axis=0, tiled=True)  25.1 us
    unnamed x23, local copies, waits for them, and re-layouts  9.11 us
    all_to_all x1, starting transfers between devices, swap_blocks(): got = lax.all_to_all(jnp.stack(pieces), name, 0, 0)  7.41 us
    dot_general x1, matrix products, cross_tower(): jnp.dot(hidden_two, ranker_final_vector, preferred_element_type=jnp.float32)  4.54 us
    dot_general x1, matrix products, item_tower(): jnp.dot(candidate_traits, candidate_tower_matrix, preferred_element_type=...  3.53 us
    gather x1, local copies, waits for them, and re-layouts, per_device(): selected_candidates = jnp.take(candidate_vectors, kept_positions, axis=0)  2.61 us
    dot_general x1, matrix products, cross_tower(): jnp.dot(cross_in, ranker_first_matrix, preferred_element_type=jnp.float32)  2.61 us
    select_n x2, other arithmetic, per_device(): selected_candidates = jnp.take(candidate_vectors, kept_positions, axis=0)  1.89 us
  transfers between devices with their start and end apart: 1, of which 0 were waited for; matrix products, arithmetic and copies ran while one was open for 1% of the time, Pallas kernels for 0%

profile of v1, /device:TPU:0, one launch (start us, length us, event | category | flops | bytes accessed | tf_op | source)
XLA Modules:
  0.0 60.7 jit_solution(2488181688227770097)
XLA Ops:
  0.6 0.0 copy-start
  0.6 0.8 %compare_and_fusion = pred[64,8]{0,1:T(8,128)(4,1)S(1)} fusion(s32[64,8]{0,1:T(8,128)} %param.10), kind=kLoop, calls=%fused_computation.50 | loop fusion | flops 3072 | bytes 2560 | tf_op jit(solution)/shard_map/jit(_take)/and | solution.py:53
  1.5 0.7 %compare_select_fusion = s32[64,8]{0,1:T(8,128)S(1)} fusion(s32[64,8]{0,1:T(8,128)} %param.10), kind=kLoop, calls=%fused_computation.48 | loop fusion | flops 1536 | bytes 4096 | tf_op jit(solution)/shard_map/jit(_take)/jit(_where)/select_n | solution.py:53
  2.2 0.1 copy.29
  2.3 0.1 copy.30
  2.4 0.1 reshape.38
  2.5 3.5 %multiply_reduce_fusion = (f32[512]{0:T(512)S(1)}, f32[512,512]{0,1:T(8,128)S(1)}) fusion(bf16[512,2048]{1,0:T(8,128)(2,1)} %param.7, bf16[2048,512]{1,0:T(8,128)(2,1)} %param.8), kind=kOutput, calls=%fused_computation.14 | convolution fusion | flops 1074265600 | bytes 5244928 | tf_op jit(solution)/shard_map/dot_general | solution.py:14
  6.0 0.1 multiply_convert_fusion.7
  6.1 0.2 copy.31
  6.4 2.6 %gather_fusion = bf16[512,512]{1,0:T(8,128)(2,1)} fusion(bf16[512,512]{1,0:T(8,128)(2,1)S(1)} %copy.31, s32[1024]{0:T(1024)S(1)} %pad_clamp_fusion), kind=kCustom, calls=%fused_computation | custom fusion | bytes 1050624 | tf_op jit(solution)/shard_map/jit(_take)/gather | solution.py:53
  9.0 0.0 copy-start.2
  9.0 0.0 copy-start.1
  9.0 1.2 %bitcast_select_fusion = bf16[64,8,512]{2,1,0:T(8,128)(2,1)S(1)} fusion(bf16[512,512]{1,0:T(8,128)(2,1)} %gather_fusion, pred[64,8]{1,0:T(8,128)(4,1)S(1)} %copy.29), kind=kLoop, calls=%fused_computation.15 | loop fusion | flops 262144 | bytes 1049088 | tf_op jit(solution)/shard_map/jit(_take)/select_n | solution.py:53
  10.2 0.6 fusion.24
  10.8 0.6 %fusion.23 = bf16[16,4,8,512]{3,2,1,0:T(8,128)(2,1)} fusion(bf16[16,4,8,512]{3,2,1,0:T(8,128)(2,1)} %fusion.24, bf16[64,8,512]{2,1,0:T(8,128)(2,1)S(1)} %bitcast_select_fusion), kind=kLoop, calls=%fused_computation.45 | loop fusion | bytes 65536
  11.4 0.6 fusion.22
  12.0 0.6 %fusion.21 = bf16[16,4,8,512]{3,2,1,0:T(8,128)(2,1)} fusion(bf16[16,4,8,512]{3,2,1,0:T(8,128)(2,1)} %fusion.22, bf16[64,8,512]{2,1,0:T(8,128)(2,1)S(1)} %bitcast_select_fusion), kind=kLoop, calls=%fused_computation.41 | loop fusion | bytes 65536
  12.6 0.6 fusion.20
  13.2 0.6 %fusion.19 = bf16[16,4,8,512]{3,2,1,0:T(8,128)(2,1)} fusion(bf16[16,4,8,512]{3,2,1,0:T(8,128)(2,1)} %fusion.20, bf16[64,8,512]{2,1,0:T(8,128)(2,1)S(1)} %bitcast_select_fusion), kind=kLoop, calls=%fused_computation.37 | loop fusion | bytes 65536
  13.8 0.6 fusion.18
  14.4 0.6 fusion.17
  15.0 0.6 %fusion.16 = bf16[16,4,8,512]{3,2,1,0:T(8,128)(2,1)} fusion(bf16[16,4,8,512]{3,2,1,0:T(8,128)(2,1)} %fusion.17, bf16[64,8,512]{2,1,0:T(8,128)(2,1)S(1)} %bitcast_select_fusion), kind=kLoop, calls=%fused_computation.31 | loop fusion | bytes 65536
  15.6 0.6 %fusion.15 = bf16[16,4,8,512]{3,2,1,0:T(8,128)(2,1)} fusion(bf16[16,4,8,512]{3,2,1,0:T(8,128)(2,1)} %fusion.16, bf16[64,8,512]{2,1,0:T(8,128)(2,1)S(1)} %bitcast_select_fusion), kind=kLoop, calls=%fused_computation.29 | loop fusion | bytes 65536
  16.3 0.6 fusion.14
  16.9 0.6 fusion.13
  17.5 0.6 fusion.12
  18.1 0.6 fusion.11
  18.7 0.6 fusion.10
  19.3 0.6 %fusion.9 = bf16[16,4,8,512]{3,2,1,0:T(8,128)(2,1)} fusion(bf16[16,4,8,512]{3,2,1,0:T(8,128)(2,1)} %fusion.10, bf16[64,8,512]{2,1,0:T(8,128)(2,1)S(1)} %bitcast_select_fusion), kind=kLoop, calls=%fused_computation.17 | loop fusion | bytes 65536 | tf_op jit(solution)/shard_map/stack | solution.py:9
  19.9 7.4 %all-to-all-start = ((bf16[16,4,8,512]{3,2,1,0:T(8,128)(2,1)}), bf16[16,4,8,512]{3,2,1,0:T(8,128)(2,1)S(1)}, u32[]{:S(2)}, u32[]{:S(2)}) async-start(bf16[16,4,8,512]{3,2,1,0:T(8,128)(2,1)} %fusion.9), calls=%async_computation | async-start | bytes 1048576 | tf_op jit(solution)/shard_map/all_to_all | solution.py:9
  27.3 0.0 copy-done.2
  27.3 0.0 copy-done.1
  27.4 25.1 %all-gather = bf16[16,4,512]{2,1,0:T(4,128)(2,1)S(1)} all-gather(bf16[1,4,512]{2,1,0:T(4,128)(2,1)S(1)} %bitcast.86), channel_id=1, replica_groups=mesh['groups'=2,'items'=16] {'items'}, dimensions={0}, use_global_device_ids=true | all-gather | bytes 69632 | tf_op jit(solution)/shard_map/all_gather | solution.py:49
  52.5 0.9 %convolution_multiply_fusion = f32[512,64]{0,1:T(8,128)} fusion(bf16[64,512]{1,0:T(8,128)(2,1)S(1)} %reshape.47, bf16[512,512]{0,1:T(8,128)(2,1)S(1)} %multiply_convert_fusion.7), kind=kOutput, calls=%fused_computation.3 | convolution fusion | flops 33587200 | bytes 720896 | tf_op jit(solution)/shard_map/dot_general | solution.py:50
  53.3 0.0 all-to-all-done
  53.4 0.1 fusion.6
  53.5 0.0 copy-done
  53.5 2.6 %fusion.2 = f32[512,1024]{1,0:T(8,128)} fusion(bf16[1024,1024]{1,0:T(8,128)(2,1)S(1)} %copy-done, bf16[512,512]{1,0:T(8,128)(2,1)S(1)} %bitcast.85, bf16[512,512]{1,0:T(8,128)(2,1)S(1)} %fusion.6), kind=kOutput, calls=%fused_computation.6 | convolution fusion | flops 1075838976 | bytes 5242880 | tf_op jit(solution)/shard_map/dot_general | solution.py:28
  56.1 4.5 %fusion.1 = f32[1,512]{1,0:T(1,128)} fusion(bf16[1024,1]{0,1:T(2,128)(2,1)S(1)} %reshape.48, bf16[1024,1024]{1,0:T(8,128)(2,1)} %param.12, f32[512,1024]{1,0:T(8,128)} %fusion.2), kind=kOutput, calls=%fused_computation.5 | convolution fusion | flops 1080033280 | bytes 4198400 | tf_op jit(solution)/shard_map/dot_general | solution.py:33
  (6 shorter events, 0.1 us)
Async XLA Ops:
  0.6 52.9 %copy-start = (bf16[1024,1024]{1,0:T(8,128)(2,1)S(1)}, bf16[1024,1024]{1,0:T(8,128)(2,1)}, u32[]{:S(2)}) copy-start(bf16[1024,1024]{1,0:T(8,128)(2,1)} %param.11) | copy-start | bytes 6291460
  9.0 18.3 %copy-start.2 = (bf16[1024]{0:T(1024)(128)(2,1)S(1)}, bf16[1024]{0:T(1024)(128)(2,1)}, u32[]{:S(2)}) copy-start(bf16[1024]{0:T(1024)(128)(2,1)} %param.13) | copy-start | bytes 6148
  9.0 18.3 %copy-start.1 = (bf16[4,512]{1,0:T(4,128)(2,1)S(1)}, bf16[4,512]{1,0:T(4,128)(2,1)}, u32[]{:S(2)}) copy-start(bf16[4,512]{1,0:T(4,128)(2,1)} %param.9) | copy-start | bytes 12292
  19.9 33.5 %all-to-all-start = ((bf16[16,4,8,512]{3,2,1,0:T(8,128)(2,1)}), bf16[16,4,8,512]{3,2,1,0:T(8,128)(2,1)S(1)}, u32[]{:S(2)}, u32[]{:S(2)}) async-start(bf16[16,4,8,512]{3,2,1,0:T(8,128)(2,1)} %fusion.9), calls=%async_computation | async-start | bytes 1048576 | tf_op jit(solution)/shard_map/all_to_all | solution.py:9
